TPU v7x, 512 devices: a whole 4x4x16 slice. The times are simulated.
512 devices in a mesh: bl: 32 (over y, x, core), dir: 16 (over z).
Axes of the slice: x: 4, y: 4, z: 16, core: 2. Of those that a mesh axis runs over, the one named last changes fastest.
Arguments:
- visibilities: float32 [8, 16, 8192], P(None, 'dir', 'bl'), may hold values from -24 to 24
- coherencies: bfloat16 [32, 8, 16, 8192], P('dir', None, None, 'bl'), may hold values from -6 to 6
- gain_offsets: float32 [32, 8, 512], P(None, None, 'bl'), may hold values from -1.5 to 1.5
- stations: int32 [2, 8192], P(None, 'bl'), may hold values from 0 to 511, as said below
- solve_order: int32 [32], replicated, may hold values from 0 to 31, each once
- counts: int32 [32], replicated, may hold values from 1 to 2
- damping: int32 [32], replicated, may hold values from 1 to 8
Outputs:
- gains: float32 [32, 8, 512], P(None, None, 'bl')
- residual: float32 [8, 16, 8192], P(None, 'dir', 'bl')
Inputs may be any that keep to these rules, and one draw needn't show every extreme that they name: Each baseline names two different stations. `solve_order`: each direction appears once.
All inputs are finite; a program needn't handle non-finite values.
Results may differ from a plain program's by a relative error of at most 0.0003.
Values may be sent and summed in bfloat16 or wider, within the bound.
A program may use at most 64 MiB of HBM per device.

v0:
```python
import jax
import jax.numpy as jnp
from jax import lax
from jax.sharding import PartitionSpec as P

LM_ITERS = 2
SOLVED = 4


def matrix_entry(mat, i, j):
    return (mat[4 * i + 2 * j], mat[4 * i + 2 * j + 1])


def matmul_two(left, right):
    pieces = []
    for i in (0, 1):
        for j in (0, 1):
            left_r0, left_i0 = matrix_entry(left, i, 0)
            left_r1, left_i1 = matrix_entry(left, i, 1)
            right_r0, right_i0 = matrix_entry(right, 0, j)
            right_r1, right_i1 = matrix_entry(right, 1, j)
            pieces.append(
                left_r0 * right_r0 - left_i0 * right_i0 + left_r1 * right_r1 - left_i1 * right_i1
            )
            pieces.append(
                left_r0 * right_i0 + left_i0 * right_r0 + left_r1 * right_i1 + left_i1 * right_r1
            )
    return jnp.stack(pieces)


def adjoint(mat):
    return jnp.stack([mat[0], -mat[1], mat[4], -mat[5], mat[2], -mat[3], mat[6], -mat[7]])


def apply_gains(gain_p, coher_now, gain_q):
    return matmul_two(matmul_two(gain_p, coher_now), adjoint(gain_q))


def gram_parts(gram):
    return jnp.stack([gram[0], gram[6], gram[2], gram[3]])


def station_terms(gain_p, gain_q, coher_now, target):
    z_rows = matmul_two(coher_now, adjoint(gain_q))
    y_rows = matmul_two(adjoint(coher_now), adjoint(gain_p))
    leading_endpoint = jnp.concatenate(
        [matmul_two(target, adjoint(z_rows)), gram_parts(matmul_two(z_rows, adjoint(z_rows)))], 0
    )
    second = jnp.concatenate(
        [
            matmul_two(adjoint(target), adjoint(y_rows)),
            gram_parts(matmul_two(y_rows, adjoint(y_rows))),
        ],
        0,
    )
    return (jnp.sum(leading_endpoint, axis=1), jnp.sum(second, axis=1))


def solve_station(gathered_sums, gain_now, damp_value):
    numerator = gathered_sums[:8] + damp_value * gain_now
    diag_a = gathered_sums[8] + damp_value
    diag_d = gathered_sums[9] + damp_value
    cross_r = gathered_sums[10]
    cross_i = gathered_sums[11]
    determinant = diag_a * diag_d - cross_r * cross_r - cross_i * cross_i
    zeros_row = jnp.zeros_like(determinant)
    inverse = (
        jnp.stack([diag_d, zeros_row, -cross_r, -cross_i, -cross_r, cross_i, diag_a, zeros_row])
        / determinant
    )
    return matmul_two(numerator, inverse)


def on_device(visibilities, coherencies, gain_offsets, stations, solve_order, counts, damping):
    identity = jnp.zeros((8,), jnp.float32).at[0].set(1.0).at[6].set(1.0)
    start = lax.all_gather(gain_offsets, "bl", axis=2, tiled=True) + identity[None, :, None]
    groups = lax.axis_size("bl")
    total_channels = coherencies.shape[2]
    station_count = start.shape[2]
    damping_factor = visibilities.shape[2] * groups * total_channels / station_count
    coher_all = lax.all_to_all(coherencies, "dir", 2, 0, tiled=True)
    ends_p = jnp.take(start, stations[0], axis=2)
    ends_q = jnp.take(start, stations[1], axis=2)
    gain_p = jnp.transpose(ends_p, (1, 0, 2))[:, :, None, :]
    gain_q = jnp.transpose(ends_q, (1, 0, 2))[:, :, None, :]
    coher_f32 = jnp.transpose(coher_all, (1, 0, 2, 3)).astype(jnp.float32)
    first_model = jnp.sum(apply_gains(gain_p, coher_f32, gain_q), axis=1)
    first_residual = visibilities - first_model

    def direction_model(gain_now, coher_now):
        gain_p = jnp.take(gain_now, stations[0], axis=1)[:, None, :]
        gain_q = jnp.take(gain_now, stations[1], axis=1)[:, None, :]
        return apply_gains(gain_p, coher_now, gain_q)

    def sweep(step_index, state):
        gain_table, residual = state
        which = solve_order[step_index]
        coher_now = lax.dynamic_index_in_dim(coher_all, which, 0, keepdims=False).astype(
            jnp.float32
        )
        damp_value = damping[which].astype(jnp.float32) * damping_factor
        gain_start = gain_table[which]
        target = residual + direction_model(gain_start, coher_now)

        def iterate(round_index, gain_now):
            gain_p = jnp.take(gain_now, stations[0], axis=1)[:, None, :]
            gain_q = jnp.take(gain_now, stations[1], axis=1)[:, None, :]
            leading_endpoint, second = station_terms(gain_p, gain_q, coher_now, target)
            local_sums = (
                jax.ops.segment_sum(leading_endpoint.T, stations[0], station_count)
                + jax.ops.segment_sum(second.T, stations[1], station_count)
            ).T
            gathered_sums = lax.psum(local_sums, ("bl", "dir"))
            return solve_station(gathered_sums, gain_now, damp_value)

        rounds = jnp.clip(counts[which], 0, LM_ITERS)
        gain_final = lax.fori_loop(0, rounds, iterate, gain_start)
        residual = target - direction_model(gain_final, coher_now)
        return (gain_table.at[which].set(gain_final), residual)

    gain_table, residual = lax.fori_loop(0, SOLVED, sweep, (start, first_residual))
    own_width = station_count // groups
    gains = lax.dynamic_slice_in_dim(gain_table, lax.axis_index("bl") * own_width, own_width, 2)
    return (gains, residual)


def solution(mesh):
    return jax.shard_map(
        on_device,
        mesh=mesh,
        in_specs=(
            P(None, "dir", "bl"),
            P("dir", None, None, "bl"),
            P(None, None, "bl"),
            P(None, "bl"),
            P(),
            P(),
            P(),
        ),
        out_specs=(P(None, None, "bl"), P(None, "dir", "bl")),
        check_vma=False,
    )
```

profile of v0, /device:TPU:1, one launch (start us, length us, event | category | flops | bytes accessed | tf_op | source)
XLA Modules:
  0.0 847.1 jit_solution(9811879134477437065)
XLA Ops:
  0.6 1.6 copy.1122
  2.2 15.7 %all-to-all-start = ((bf16[2,8,16,256]{3,1,0,2:T(8,128)(2,1)}), bf16[2,8,16,256]{3,1,0,2:T(8,128)(2,1)S(1)}, u32[]{:S(2)}, u32[]{:S(2)}) async-start(bf16[2,8,16,256]{3,1,0,2:T(8,128)(2,1)} %copy.1122), calls=%async_computation | async-start | bytes 262144 | tf_op jit(solution)/shard_map/all_to_all | solution.py:81
  19.7 27.2 %all_gather.3 = f32[32,8,512]{0,1,2:T(8,128)S(1)} all-gather(f32[32,8,16]{0,1,2:T(8,128)S(1)} %copy.1120), channel_id=1, replica_groups=mesh['bl'=32,'dir'=16] {'bl'}, dimensions={2}, use_global_device_ids=true | all-gather | bytes 540672 | tf_op jit(solution)/shard_map/all_gather | solution.py:76
  48.0 2.0 gather_fusion.7
  50.0 1.6 copy.1124
  51.6 2.0 gather_fusion.6
  53.6 1.6 copy.1121
  57.4 788.4 %while.42 = (s32[]{:T(128)}, f32[32,8,512]{2,1,0:T(8,128)S(1)}, f32[8,1,256]{2,1,0:T(1,128)S(1)}, s32[32]{0:T(128)S(1)}, s32[32]{0:T(128)S(1)}, /*index=5*/bf16[...) while((s32[]{:T(128)}, f32[32,8,512]{2,1,0:T(8,128)S(1)}, ...), condition=%wide.region_8.12_spmd, body=%wide.region_1.11_spmd.sunk | while | flops 253464 | bytes 1958014 | solution.py:121
  64.8 109.2 %while.43 = (s32[]{:T(128)}, f32[8,512]{1,0:T(8,128)S(1)}, s32[]{:T(128)}, s32[2,256]{1,0:T(2,128)S(1)}, f32[8,1,256]{2,1,0:T(1,128)S(1)}, /*index=5*/f32[8,1,25...) while((s32[]{:T(128)}, f32[8,512]{1,0:T(8,128)S(1)}, ...), condition=%wide.region_7.10_spmd, body=%wide.region_3.9_spmd.sunk | while | flops 160768 | bytes 1263793 | solution.py:117
  67.0 1.5 scatter_custom_fusion.11
  69.0 1.5 scatter_custom_fusion.10
  70.6 103.1 %psum.9 = f32[12,512]{1,0:T(8,128)S(1)} all-reduce(f32[12,512]{1,0:T(8,128)S(1)} %add_bitcast_fusion.2), channel_id=1, replica_groups=mesh['bl'=32,'dir'=16] {'bl','dir'}, use_global_device_ids=true, to_apply=%region_6.8 | all-reduce | flops 6144 | bytes 49152 | tf_op jit(solution)/shard_map/while/body/eval_jaxpr/while/body/psum | solution.py:113
  184.6 212.3 %while.43 = (s32[]{:T(128)}, f32[8,512]{1,0:T(8,128)S(1)}, s32[]{:T(128)}, s32[2,256]{1,0:T(2,128)S(1)}, f32[8,1,256]{2,1,0:T(1,128)S(1)}, /*index=5*/f32[8,1,25...) while((s32[]{:T(128)}, f32[8,512]{1,0:T(8,128)S(1)}, ...), condition=%wide.region_7.10_spmd, body=%wide.region_3.9_spmd.sunk | while | flops 160768 | bytes 1263793 | solution.py:117
  186.8 1.5 scatter_custom_fusion.11
  188.8 1.5 scatter_custom_fusion.10
  190.4 100.7 %psum.9 = f32[12,512]{1,0:T(8,128)S(1)} all-reduce(f32[12,512]{1,0:T(8,128)S(1)} %add_bitcast_fusion.2), channel_id=1, replica_groups=mesh['bl'=32,'dir'=16] {'bl','dir'}, use_global_device_ids=true, to_apply=%region_6.8 | all-reduce | flops 6144 | bytes 49152 | tf_op jit(solution)/shard_map/while/body/eval_jaxpr/while/body/psum | solution.py:113
  293.6 1.5 scatter_custom_fusion.11
  295.5 1.5 scatter_custom_fusion.10
  297.2 99.4 %psum.9 = f32[12,512]{1,0:T(8,128)S(1)} all-reduce(f32[12,512]{1,0:T(8,128)S(1)} %add_bitcast_fusion.2), channel_id=1, replica_groups=mesh['bl'=32,'dir'=16] {'bl','dir'}, use_global_device_ids=true, to_apply=%region_6.8 | all-reduce | flops 6144 | bytes 49152 | tf_op jit(solution)/shard_map/while/body/eval_jaxpr/while/body/psum | solution.py:113
  407.5 212.1 %while.43 = (s32[]{:T(128)}, f32[8,512]{1,0:T(8,128)S(1)}, s32[]{:T(128)}, s32[2,256]{1,0:T(2,128)S(1)}, f32[8,1,256]{2,1,0:T(1,128)S(1)}, /*index=5*/f32[8,1,25...) while((s32[]{:T(128)}, f32[8,512]{1,0:T(8,128)S(1)}, ...), condition=%wide.region_7.10_spmd, body=%wide.region_3.9_spmd.sunk | while | flops 160768 | bytes 1263793 | solution.py:117
  409.7 1.5 scatter_custom_fusion.11
  411.7 1.5 scatter_custom_fusion.10
  413.3 100.4 %psum.9 = f32[12,512]{1,0:T(8,128)S(1)} all-reduce(f32[12,512]{1,0:T(8,128)S(1)} %add_bitcast_fusion.2), channel_id=1, replica_groups=mesh['bl'=32,'dir'=16] {'bl','dir'}, use_global_device_ids=true, to_apply=%region_6.8 | all-reduce | flops 6144 | bytes 49152 | tf_op jit(solution)/shard_map/while/body/eval_jaxpr/while/body/psum | solution.py:113
  516.2 1.5 scatter_custom_fusion.11
  518.1 1.5 scatter_custom_fusion.10
  519.7 99.6 %psum.9 = f32[12,512]{1,0:T(8,128)S(1)} all-reduce(f32[12,512]{1,0:T(8,128)S(1)} %add_bitcast_fusion.2), channel_id=1, replica_groups=mesh['bl'=32,'dir'=16] {'bl','dir'}, use_global_device_ids=true, to_apply=%region_6.8 | all-reduce | flops 6144 | bytes 49152 | tf_op jit(solution)/shard_map/while/body/eval_jaxpr/while/body/psum | solution.py:113
  630.2 212.2 %while.43 = (s32[]{:T(128)}, f32[8,512]{1,0:T(8,128)S(1)}, s32[]{:T(128)}, s32[2,256]{1,0:T(2,128)S(1)}, f32[8,1,256]{2,1,0:T(1,128)S(1)}, /*index=5*/f32[8,1,25...) while((s32[]{:T(128)}, f32[8,512]{1,0:T(8,128)S(1)}, ...), condition=%wide.region_7.10_spmd, body=%wide.region_3.9_spmd.sunk | while | flops 160768 | bytes 1263793 | solution.py:117
  632.5 1.5 scatter_custom_fusion.11
  634.4 1.5 scatter_custom_fusion.10
  636.0 100.5 %psum.9 = f32[12,512]{1,0:T(8,128)S(1)} all-reduce(f32[12,512]{1,0:T(8,128)S(1)} %add_bitcast_fusion.2), channel_id=1, replica_groups=mesh['bl'=32,'dir'=16] {'bl','dir'}, use_global_device_ids=true, to_apply=%region_6.8 | all-reduce | flops 6144 | bytes 49152 | tf_op jit(solution)/shard_map/while/body/eval_jaxpr/while/body/psum | solution.py:113
  739.0 1.5 scatter_custom_fusion.11
  742.5 99.6 %psum.9 = f32[12,512]{1,0:T(8,128)S(1)} all-reduce(f32[12,512]{1,0:T(8,128)S(1)} %add_bitcast_fusion.2), channel_id=1, replica_groups=mesh['bl'=32,'dir'=16] {'bl','dir'}, use_global_device_ids=true, to_apply=%region_6.8 | all-reduce | flops 6144 | bytes 49152 | tf_op jit(solution)/shard_map/while/body/eval_jaxpr/while/body/psum | solution.py:113
  (595 shorter events, 56.4 us)
Async XLA Ops:
  0.6 46.2 %copy-start.4 = (f32[8]{0:T(128)S(1)}, f32[8]{0:T(128)}, u32[]{:S(2)}) copy-start(f32[8]{0:T(128)} %constant.188.clone.1) | copy-start | bytes 100
  2.2 53.1 %all-to-all-start = ((bf16[2,8,16,256]{3,1,0,2:T(8,128)(2,1)}), bf16[2,8,16,256]{3,1,0,2:T(8,128)(2,1)S(1)}, u32[]{:S(2)}, u32[]{:S(2)}) async-start(bf16[2,8,16,256]{3,1,0,2:T(8,128)(2,1)} %copy.1122), calls=%async_computation | async-start | bytes 262144 | tf_op jit(solution)/shard_map/all_to_all | solution.py:81
  55.2 2.1 copy-start.3
  55.2 2.1 copy-start
  55.3 2.1 copy-start.2
  55.3 2.1 copy-start.5
  55.3 2.1 copy-start.6
  55.3 2.1 copy-start.7
  845.8 1.3 copy-start.1
where the time goes:
time: 849 us; the launch traced here: 847 us
  blocking collectives  731 us (86%)
  local copies, waits for them, and re-layouts  49.5 us (6%)
  other arithmetic  35.1 us (4%)
  starting transfers between devices  15.7 us (2%)
  loops' own time  15.3 us (2%)
    psum x7, blocking collectives, iterate(): gathered_sums = lax.psum(local_sums, ('bl', 'dir'))  703 us
    all_gather x1, blocking collectives, on_device(): lax.all_gather(gain_offsets, 'bl', axis=2, tiled=True)  27.2 us
  transfers between devices with their start and end apart: 1, of which 0 were waited for; matrix products, arithmetic and copies ran while one was open for 1% of the time, Pallas kernels for 0%

commit v1 on v0

--- a/solution.py
+++ b/solution.py
@@ -110,7 +110,11 @@
                 jax.ops.segment_sum(leading_endpoint.T, stations[0], station_count)
                 + jax.ops.segment_sum(second.T, stations[1], station_count)
             ).T
-            gathered_sums = lax.psum(local_sums, ("bl", "dir"))
+
+            def move_the_panel(local):
+                return jnp.sum(lax.all_gather(local, axis_name=("bl", "dir")), axis=0)
+
+            gathered_sums = move_the_panel(local_sums)
             return solve_station(gathered_sums, gain_now, damp_value)
 
         rounds = jnp.clip(counts[which], 0, LM_ITERS)

time: 849 us -> 1720 us (2.03)
  waiting for transfers between devices: 0.01 us -> 1510 us
  blocking collectives: 731 us -> 27.2 us
  other arithmetic: 35.1 us -> 82 us
    all_gather x0 -> x7, waiting for transfers between devices: none -> 1510 us  [move_the_panel(): return jnp.sum(lax.all_gather(local, axis_name=('bl', 'dir')), axis=0)]
    psum x7 -> x0, blocking collectives: 703 us -> none  [iterate(): gathered_sums = lax.psum(local_sums, ('bl', 'dir'))]
    reduce_sum x0 -> x7, other arithmetic: none -> 47.2 us  [move_the_panel(): return jnp.sum(lax.all_gather(local, axis_name=('bl', 'dir')), axis=0)]
  transfers between devices with their start and end apart: 1 -> 8, of which waited for: 0 -> 7; matrix products, arithmetic and copies ran while one was open for 1% -> 1% of each run, Pallas kernels for 0% -> 0%
where the time goes in v1:
time: 1720 us
  waiting for transfers between devices  1510 us (88%)
  other arithmetic  82 us (5%)
  local copies, waits for them, and re-layouts  52.7 us (3%)
  blocking collectives  27.2 us (2%)
    all_gather x7, waiting for transfers between devices, move_the_panel(): return jnp.sum(lax.all_gather(local, axis_name=('bl', 'dir')), axis=0)  1510 us
    reduce_sum x7, other arithmetic, move_the_panel(): return jnp.sum(lax.all_gather(local, axis_name=('bl', 'dir')), axis=0)  47.2 us
  transfers between devices with their start and end apart: 8, of which 7 were waited for; matrix products, arithmetic and copies ran while one was open for 1% of the time, Pallas kernels for 0%

profile of v1, /device:TPU:1, one launch (start us, length us, event | category | flops | bytes accessed | tf_op | source)
XLA Modules:
  0.0 1719.9 jit_solution(1394755886773002978)
XLA Ops:
  7.2 1.6 copy.697
  8.8 15.7 all-to-all-start
  26.2 27.2 %all_gather.11 = f32[32,8,512]{0,1,2:T(8,128)S(1)} all-gather(f32[32,8,16]{0,1,2:T(8,128)S(1)} %copy.695), channel_id=1, replica_groups=mesh['bl'=32,'dir'=16] {'bl'}, dimensions={2}, use_global_device_ids=true | all-gather | bytes 540672 | tf_op jit(solution)/shard_map/all_gather | solution.py:76
  54.5 2.0 gather_fusion.7
  56.6 1.6 copy.699
  58.1 2.0 gather_fusion.6
  60.2 1.6 copy.696
  64.0 1647.8 %while.42 = (s32[]{:T(128)}, f32[32,8,512]{2,1,0:T(8,128)S(1)}, f32[8,1,256]{2,1,0:T(1,128)S(1)}, s32[32]{0:T(128)S(1)}, s32[32]{0:T(128)S(1)}, /*index=5*/bf16[...) while((s32[]{:T(128)}, f32[32,8,512]{2,1,0:T(8,128)S(1)}, ...), condition=%wide.region_8.12_spmd, body=%wide.region_1.11_spmd.sunk | while | flops 3386904 | bytes 56492200 | solution.py:125
  71.3 232.4 %while.43 = (s32[]{:T(128)}, f32[8,512]{1,0:T(8,128)S(1)}, s32[]{:T(128)}, s32[2,256]{1,0:T(2,128)S(1)}, f32[8,1,256]{2,1,0:T(1,128)S(1)}, /*index=5*/f32[8,1,25...) while((s32[]{:T(128)}, f32[8,512]{1,0:T(8,128)S(1)}, ...), condition=%wide.region_7.10_spmd, body=%wide.region_3.9_spmd.sunk | while | flops 3294208 | bytes 55797980 | solution.py:121
  75.4 1.5 scatter_custom_fusion.10
  77.7 219.0 %all-gather.6.cloned.1.call-done = f32[512,12,512]{2,1,0:T(8,128)} async-done(((f32[1,12,512]{2,1,0:T(8,128)}), f32[512,12,512]{2,1,0:T(8,128)}) %all-gather.6.cloned.1.call-update) | async-done | bytes 12582928 | tf_op jit(solution)/shard_map/while/body/eval_jaxpr/while/body/all_gather | solution.py:115
  296.7 6.7 reduce_sum.37
  314.1 457.8 %while.43 = (s32[]{:T(128)}, f32[8,512]{1,0:T(8,128)S(1)}, s32[]{:T(128)}, s32[2,256]{1,0:T(2,128)S(1)}, f32[8,1,256]{2,1,0:T(1,128)S(1)}, /*index=5*/f32[8,1,25...) while((s32[]{:T(128)}, f32[8,512]{1,0:T(8,128)S(1)}, ...), condition=%wide.region_7.10_spmd, body=%wide.region_3.9_spmd.sunk | while | flops 3294208 | bytes 55797980 | solution.py:121
  318.2 1.5 scatter_custom_fusion.10
  320.5 215.5 %all-gather.6.cloned.1.call-done = f32[512,12,512]{2,1,0:T(8,128)} async-done(((f32[1,12,512]{2,1,0:T(8,128)}), f32[512,12,512]{2,1,0:T(8,128)}) %all-gather.6.cloned.1.call-update) | async-done | bytes 12582928 | tf_op jit(solution)/shard_map/while/body/eval_jaxpr/while/body/all_gather | solution.py:115
  536.0 6.7 reduce_sum.37
  547.1 1.5 scatter_custom_fusion.10
  549.4 215.5 %all-gather.6.cloned.1.call-done = f32[512,12,512]{2,1,0:T(8,128)} async-done(((f32[1,12,512]{2,1,0:T(8,128)}), f32[512,12,512]{2,1,0:T(8,128)}) %all-gather.6.cloned.1.call-update) | async-done | bytes 12582928 | tf_op jit(solution)/shard_map/while/body/eval_jaxpr/while/body/all_gather | solution.py:115
  764.9 6.7 reduce_sum.37
  782.4 457.8 %while.43 = (s32[]{:T(128)}, f32[8,512]{1,0:T(8,128)S(1)}, s32[]{:T(128)}, s32[2,256]{1,0:T(2,128)S(1)}, f32[8,1,256]{2,1,0:T(1,128)S(1)}, /*index=5*/f32[8,1,25...) while((s32[]{:T(128)}, f32[8,512]{1,0:T(8,128)S(1)}, ...), condition=%wide.region_7.10_spmd, body=%wide.region_3.9_spmd.sunk | while | flops 3294208 | bytes 55797980 | solution.py:121
  786.5 1.5 scatter_custom_fusion.10
  788.8 215.5 %all-gather.6.cloned.1.call-done = f32[512,12,512]{2,1,0:T(8,128)} async-done(((f32[1,12,512]{2,1,0:T(8,128)}), f32[512,12,512]{2,1,0:T(8,128)}) %all-gather.6.cloned.1.call-update) | async-done | bytes 12582928 | tf_op jit(solution)/shard_map/while/body/eval_jaxpr/while/body/all_gather | solution.py:115
  1004.3 6.7 reduce_sum.37
  1015.4 1.5 scatter_custom_fusion.10
  1017.7 215.5 %all-gather.6.cloned.1.call-done = f32[512,12,512]{2,1,0:T(8,128)} async-done(((f32[1,12,512]{2,1,0:T(8,128)}), f32[512,12,512]{2,1,0:T(8,128)}) %all-gather.6.cloned.1.call-update) | async-done | bytes 12582928 | tf_op jit(solution)/shard_map/while/body/eval_jaxpr/while/body/all_gather | solution.py:115
  1233.2 6.7 reduce_sum.37
  1250.6 457.8 %while.43 = (s32[]{:T(128)}, f32[8,512]{1,0:T(8,128)S(1)}, s32[]{:T(128)}, s32[2,256]{1,0:T(2,128)S(1)}, f32[8,1,256]{2,1,0:T(1,128)S(1)}, /*index=5*/f32[8,1,25...) while((s32[]{:T(128)}, f32[8,512]{1,0:T(8,128)S(1)}, ...), condition=%wide.region_7.10_spmd, body=%wide.region_3.9_spmd.sunk | while | flops 3294208 | bytes 55797980 | solution.py:121
  1257.0 215.5 %all-gather.6.cloned.1.call-done = f32[512,12,512]{2,1,0:T(8,128)} async-done(((f32[1,12,512]{2,1,0:T(8,128)}), f32[512,12,512]{2,1,0:T(8,128)}) %all-gather.6.cloned.1.call-update) | async-done | bytes 12582928 | tf_op jit(solution)/shard_map/while/body/eval_jaxpr/while/body/all_gather | solution.py:115
  1472.5 6.7 reduce_sum.37
  1483.6 1.5 scatter_custom_fusion.10
  1485.9 215.5 %all-gather.6.cloned.1.call-done = f32[512,12,512]{2,1,0:T(8,128)} async-done(((f32[1,12,512]{2,1,0:T(8,128)}), f32[512,12,512]{2,1,0:T(8,128)}) %all-gather.6.cloned.1.call-update) | async-done | bytes 12582928 | tf_op jit(solution)/shard_map/while/body/eval_jaxpr/while/body/all_gather | solution.py:115
  1701.4 6.7 reduce_sum.37
  (609 shorter events, 70.1 us)
Async XLA Ops:
  7.2 46.2 %copy-start.4 = (f32[8]{0:T(128)S(1)}, f32[8]{0:T(128)}, u32[]{:S(2)}) copy-start(f32[8]{0:T(128)} %constant.188.clone.1) | copy-start | bytes 100
  8.8 53.1 %all-to-all-start = ((bf16[2,8,16,256]{3,1,0,2:T(8,128)(2,1)}), bf16[2,8,16,256]{3,1,0,2:T(8,128)(2,1)S(1)}, u32[]{:S(2)}, u32[]{:S(2)}) async-start(bf16[2,8,16,256]{3,1,0,2:T(8,128)(2,1)} %copy.697), calls=%async_computation | async-start | bytes 262144 | tf_op jit(solution)/shard_map/all_to_all | solution.py:81
  61.8 2.1 copy-start.3
  61.8 2.1 copy-start
  61.8 2.1 copy-start.2
  61.8 2.1 copy-start.5
  61.8 2.1 copy-start.6
  61.8 2.1 copy-start.7
  71.3 225.4 %all-gather.6.cloned.1.call-start = ((), (), s32[]{:S(2)}) async-start(), calls=%async_computation.1 | async-start | bytes 16809984 | tf_op jit(solution)/shard_map/while/body/eval_jaxpr/while/body/all_gather | solution.py:115
  314.1 221.9 %all-gather.6.cloned.1.call-start = ((), (), s32[]{:S(2)}) async-start(), calls=%async_computation.1 | async-start | bytes 16809984 | tf_op jit(solution)/shard_map/while/body/eval_jaxpr/while/body/all_gather | solution.py:115
  543.0 221.9 %all-gather.6.cloned.1.call-start = ((), (), s32[]{:S(2)}) async-start(), calls=%async_computation.1 | async-start | bytes 16809984 | tf_op jit(solution)/shard_map/while/body/eval_jaxpr/while/body/all_gather | solution.py:115
  782.4 221.9 %all-gather.6.cloned.1.call-start = ((), (), s32[]{:S(2)}) async-start(), calls=%async_computation.1 | async-start | bytes 16809984 | tf_op jit(solution)/shard_map/while/body/eval_jaxpr/while/body/all_gather | solution.py:115
  1011.3 221.9 %all-gather.6.cloned.1.call-start = ((), (), s32[]{:S(2)}) async-start(), calls=%async_computation.1 | async-start | bytes 16809984 | tf_op jit(solution)/shard_map/while/body/eval_jaxpr/while/body/all_gather | solution.py:115
  1250.7 221.9 %all-gather.6.cloned.1.call-start = ((), (), s32[]{:S(2)}) async-start(), calls=%async_computation.1 | async-start | bytes 16809984 | tf_op jit(solution)/shard_map/while/body/eval_jaxpr/while/body/all_gather | solution.py:115
  1479.6 221.9 %all-gather.6.cloned.1.call-start = ((), (), s32[]{:S(2)}) async-start(), calls=%async_computation.1 | async-start | bytes 16809984 | tf_op jit(solution)/shard_map/while/body/eval_jaxpr/while/body/all_gather | solution.py:115
  1711.8 1.3 copy-start.1
Sparse Core Ops, SparseCore 0:
  77.8 218.8 all-gather.5
  320.6 215.3 all-gather.5
  549.5 215.3 all-gather.5
  788.9 215.3 all-gather.5
  1017.8 215.3 all-gather.5
  1257.2 215.3 all-gather.5
  1486.1 215.3 all-gather.5
